TPU v7x, 32 devices: a whole 2x2x4 slice. The times are simulated.
32 devices in a mesh: groups: 2 (over x), worker: 2 (over core), tensor: 8 (over z, y).
Axes of the slice: x: 2, y: 2, z: 4, core: 2. Of those that a mesh axis runs over, the one named last changes fastest.
Arguments:
- tokens: bfloat16 [1024, 8192], P(('groups', 'worker'), 'tensor'), parts along dimension 0, may hold values from -6 to 6
- norm_gain: float32 [8192], replicated, may hold values from 0.5 to 1.5
- query_weight: bfloat16 [8192, 8192], P(None, 'tensor'), may hold values from -0.0625 to 0.0625
- key_weight: bfloat16 [8192, 1024], P(None, 'tensor'), may hold values from -0.15625 to 0.15625
- value_weight: bfloat16 [8192, 1024], P(None, 'tensor'), may hold values from -0.0625 to 0.0625
- output_weight: bfloat16 [8192, 8192], P('tensor'), may hold values from -0.0625 to 0.0625
- cached_blocks: bfloat16 [8, 1024, 2, 1024], P(('groups', 'worker'), 'tensor'), parts along dimension 0
- cache_length: int32 [8], P('groups'), parts along dimension 0, may hold values from 256 to 1024, as said below
- block_table: int32 [8, 64], P('groups'), parts along dimension 0, may hold values from 0 to 63, each once within a row
- destination: int32 [8], P('groups'), parts along dimension 0, may hold values from 0 to 1, as said below
Outputs:
- attended: bfloat16 [4, 3, 128, 8192], P(('groups', 'worker'), None, None, 'tensor'), parts along dimension 0
There are 2 independent parts, one for each index of `groups`. A program takes and returns all parts, laid end to end along the dimension named above; an argument that names none is the same for every part. Nothing has to cross between parts.
Inputs may be any that keep to these rules, and one draw needn't show every extreme that they name: Exactly 3 sequences have one destination, the others the other; which one is drawn. `cache_length`: some sequence has exactly 1024 cached tokens.
All inputs are finite; a program needn't handle non-finite values.
Results may differ from a plain program's by a relative error of at most 0.02.
The roundings to bfloat16 on the way count: a program that leaves them out, or rounds other values in their place, can miss the bound.
Values may be sent and summed in bfloat16 or wider, within the bound.
No kernel may reach another device: no remote copies, remote signals or barrier semaphores. Data moves between devices by JAX's collectives and lax.ppermute only.
A program may use at most 128 MiB of HBM per device.

v0:
```python
import math
import jax
import jax.numpy as jnp
from jax import lax
from jax.sharding import PartitionSpec as P

D = 8192
KVH = 8
HD = 128
NEW = 128
BLK = 16
CAP = 3
epsilon = 1e-05


def from_partner(block, axis, bit):
    count = lax.axis_size(axis)
    route = []
    for low in range(count):
        high = low | 1 << bit
        if high != low and high < count:
            route += [(low, high), (high, low)]
    return lax.ppermute(block, axis, route)


def rotate(values, positions):
    halfway = HD // 2
    inverse = 500000.0 ** (-(jnp.arange(halfway, dtype=jnp.float32) * 2.0 / HD))
    angles = positions[:, None] * inverse[None, :]
    cosine_table = jnp.concatenate([jnp.cos(angles), jnp.cos(angles)], axis=-1)[:, None, :]
    sine_table = jnp.concatenate([jnp.sin(angles), jnp.sin(angles)], axis=-1)[:, None, :]
    turned = jnp.concatenate([-values[..., halfway:], values[..., :halfway]], axis=-1)
    return values * cosine_table + turned * sine_table


def attend(
    token_rows,
    blocks,
    lengths,
    tables,
    norm_gain,
    query_weight,
    key_weight,
    value_weight,
    output_weight,
):
    tensor_count = lax.axis_size("tensor")
    tensor_index = lax.axis_index("tensor")
    group_width = tensor_count // KVH
    bit_count = group_width.bit_length() - 1
    seq_count = blocks.shape[0]
    total = token_rows.shape[0]
    query_cols = query_weight.shape[1]
    widened = lax.all_gather(token_rows, "tensor", axis=1, tiled=True).astype(jnp.float32)
    scaled = (widened * norm_gain[None, :]).astype(jnp.bfloat16)
    query_sum = jnp.dot(scaled, query_weight, preferred_element_type=jnp.float32)
    key_sum = jnp.dot(scaled, key_weight, preferred_element_type=jnp.float32)
    value_sum = jnp.dot(scaled, value_weight, preferred_element_type=jnp.float32)
    squares = jnp.sum(widened * widened, axis=1)
    factor = lax.rsqrt(squares / D + epsilon)[:, None]
    positions = (
        (lengths[:, None] + jnp.arange(NEW, dtype=jnp.int32)[None, :])
        .reshape(total)
        .astype(jnp.float32)
    )
    heads_here = query_cols // HD
    queries = rotate((query_sum * factor).reshape(total, heads_here, HD), positions).astype(
        jnp.bfloat16
    )
    key_full = (key_sum * factor).astype(jnp.bfloat16)
    value_full = (value_sum * factor).astype(jnp.bfloat16)
    for bit in range(bit_count):
        other_key, other_value = from_partner((key_full, value_full), "tensor", bit)
        upper = tensor_index // (1 << bit) % 2 == 1
        key_full = jnp.where(
            upper,
            jnp.concatenate([other_key, key_full], axis=1),
            jnp.concatenate([key_full, other_key], axis=1),
        )
        value_full = jnp.where(
            upper,
            jnp.concatenate([other_value, value_full], axis=1),
            jnp.concatenate([value_full, other_value], axis=1),
        )
    new_key = rotate(key_full.astype(jnp.float32)[:, None, :], positions)[:, 0, :].astype(
        jnp.bfloat16
    )
    fresh_keys = new_key.reshape(seq_count, NEW, HD)
    fresh_values = value_full.reshape(seq_count, NEW, HD)
    local_tokens = blocks.shape[1]
    inverse_root = 1.0 / math.sqrt(HD)
    query_blocks = queries.reshape(seq_count, NEW, heads_here, HD)
    causal = jnp.arange(NEW)[:, None] >= jnp.arange(NEW)[None, :]
    spread = jnp.repeat(
        blocks.reshape(seq_count, local_tokens, 2, KVH, HD), tensor_count // KVH, axis=3
    )
    arrived = lax.all_to_all(spread, "tensor", split_axis=3, concat_axis=1, tiled=True)
    context = arrived.shape[1]
    old_key = arrived[:, :, 0, 0, :]
    old_value = arrived[:, :, 1, 0, :]
    stored = jnp.arange(context, dtype=jnp.int32)
    logical = jnp.take(tables, stored // BLK, axis=1) * BLK + stored % BLK
    visible = logical < lengths[:, None]
    old_scores = (
        jnp.einsum("sqhd,skd->shqk", query_blocks, old_key, preferred_element_type=jnp.float32)
        * inverse_root
    )
    old_scores = jnp.where(visible[:, None, None, :], old_scores, -1e30)
    new_scores = (
        jnp.einsum("sqhd,skd->shqk", query_blocks, fresh_keys, preferred_element_type=jnp.float32)
        * inverse_root
    )
    new_scores = jnp.where(causal[None, None], new_scores, -1e30)
    largest = jnp.maximum(jnp.max(old_scores, axis=3), jnp.max(new_scores, axis=3))[..., None]
    old_expo = jnp.exp(old_scores - largest)
    new_expo = jnp.exp(new_scores - largest)
    denominator = (jnp.sum(old_expo, axis=3) + jnp.sum(new_expo, axis=3))[..., None]
    old_probs = (old_expo / denominator).astype(jnp.bfloat16)
    new_probs = (new_expo / denominator).astype(jnp.bfloat16)
    mixture = jnp.einsum("shqk,skd->sqhd", old_probs, old_value, preferred_element_type=jnp.float32)
    mixture = mixture + jnp.einsum(
        "shqk,skd->sqhd", new_probs, fresh_values, preferred_element_type=jnp.float32
    )
    attended_rows = mixture.astype(jnp.bfloat16).reshape(total, heads_here * HD)
    partial_value = jnp.dot(attended_rows, output_weight, preferred_element_type=jnp.float32)
    summed = lax.psum_scatter(partial_value, "tensor", scatter_dimension=1, tiled=True)
    return summed.astype(jnp.bfloat16)


def local(
    tokens,
    norm_gain,
    query_weight,
    key_weight,
    value_weight,
    output_weight,
    cached_blocks,
    cache_length,
    block_table,
    destination,
):
    worker_index = lax.axis_index("worker")
    seq_total = destination.shape[0]
    belongs = (destination == worker_index).astype(jnp.int32)
    ranking = jnp.cumsum(belongs) - 1
    matched = (belongs[None, :] == 1) & (
        ranking[None, :] == jnp.arange(CAP, dtype=jnp.int32)[:, None]
    )
    slot_owner = jnp.sum(
        matched.astype(jnp.int32) * jnp.arange(seq_total, dtype=jnp.int32)[None, :], axis=1
    )
    occupied = jnp.any(matched, axis=1)
    local_count = cached_blocks.shape[0]
    owned = worker_index * local_count + jnp.arange(local_count, dtype=jnp.int32)
    mixed = attend(
        tokens,
        cached_blocks,
        jnp.take(cache_length, owned),
        jnp.take(block_table, owned, axis=0),
        norm_gain,
        query_weight,
        key_weight,
        value_weight,
        output_weight,
    )
    everyone = lax.all_gather(mixed, "worker", axis=0, tiled=True)
    placed = jnp.take(everyone.reshape(seq_total, NEW, -1), slot_owner, axis=0)
    result = jnp.where(occupied[:, None, None], placed, jnp.zeros_like(placed))
    return result[None]


def solution(mesh):
    placed = (
        P(("groups", "worker"), "tensor"),
        P(),
        P(None, "tensor"),
        P(None, "tensor"),
        P(None, "tensor"),
        P("tensor", None),
        P(("groups", "worker"), "tensor", None, None),
        P("groups"),
        P("groups", None),
        P("groups"),
    )
    return jax.shard_map(
        local,
        mesh=mesh,
        in_specs=placed,
        out_specs=P(("groups", "worker"), None, None, "tensor"),
        check_vma=False,
    )
```

profile of v0, /device:TPU:0, one launch (start us, length us, event | category | flops | bytes accessed | tf_op | source)
XLA Modules:
  0.0 310.5 jit_solution(4129475814052174620)
XLA Ops:
  6.5 0.7 all-gather.3.cloned.1.call-update
  7.3 2.6 copy.86
  9.8 1.3 copy.87
  11.1 7.3 %all-to-all-start = ((bf16[2,128,2,8,128]{4,1,0,2,3:T(8,128)(2,1)}), bf16[2,128,2,8,128]{4,1,0,2,3:T(8,128)(2,1)S(1)}, u32[]{:S(2)}, u32[]{:S(2)}) async-start(bf16[2,128,2,8,128]{4,1,0,2,3:T(8,128)(2,1)} %copy.87), calls=%async_computation | async-start | bytes 2097152 | tf_op jit(solution)/shard_map/all_to_all | solution.py:97
  18.5 1.3 gather_fusion.2
  19.8 1.3 gather_fusion
  21.3 4.0 %gather_fusion.1 = s32[1024,2]{1,0:T(8,128)} fusion(s32[2,64]{0,1:T(8,128)S(1)} %copy.80, s32[1024]{0:T(1024)S(1)} %broadcast_clamp_fusion), kind=kCustom, calls=%fused_computation.1 | custom fusion | bytes 20480 | tf_op jit(solution)/shard_map/jit(_take)/gather | solution.py:102
  25.3 1.2 copy.81
  26.6 0.6 iota_compare_fusion
  27.3 0.5 multiply_cosine_fusion
  28.3 32.7 %all-to-all-done = bf16[2,128,2,8,128]{4,1,0,2,3:T(8,128)(2,1)S(1)} async-done(((bf16[2,128,2,8,128]{4,1,0,2,3:T(8,128)(2,1)}), bf16[2,128,2,8,128]{4,1,0,2,3:T(8,128)(2,1)S(1)}, u32[]{:S(2)}, u32[]{:S(2)}) %all-to-all-start) | async-done | bytes 1048608 | tf_op jit(solution)/shard_map/all_to_all | solution.py:97
  61.1 1.0 copy.88
  62.1 40.3 %all-gather.3.cloned.1.call-done = bf16[256,8192]{1,0:T(8,128)(2,1)} async-done(((bf16[256,1024]{1,0:T(8,128)(2,1)}), bf16[256,8192]{1,0:T(8,128)(2,1)}) %all-gather.3.cloned.1.call-update) | async-done | bytes 4194320 | tf_op jit(solution)/shard_map/all_gather | solution.py:54
  102.4 3.1 fusion.1
  105.5 3.6 %fusion.25 = bf16[256,128]{0,1:T(8,128)(2,1)S(1)} fusion(bf16[8192,128]{1,0:T(8,128)(2,1)S(1)} %copy-done, bf16[256,8192]{1,0:T(8,128)(2,1)} %all-gather.3.cloned.1.call-done, f32[8192]{0:T(1024)} %param.11, f32[256]{0:T(256)S(1)} %add_rsqrt_fusion), kind=kOutput, calls=%fused_computation.28 | convolution fusion | flops 543227904 | bytes 6390784 | tf_op jit(solution)/shard_map/dot_general | solution.py:58
  109.1 0.6 reshape.302
  109.7 4.3 %fusion.31 = f32[256,128]{0,1:T(8,128)S(1)} fusion(bf16[8192,128]{1,0:T(8,128)(2,1)} %param.13, bf16[256,8192]{1,0:T(8,128)(2,1)} %all-gather.3.cloned.1.call-done, f32[8192]{0:T(1024)S(1)} %copy-done.6, f32[256]{0:T(256)S(1)} %add_rsqrt_fusion), kind=kOutput, calls=%fused_computation.30 | convolution fusion | flops 543260672 | bytes 6456320 | tf_op jit(solution)/shard_map/dot_general | solution.py:57
  114.2 9.5 %fusion.11 = f32[256,1024]{1,0:T(8,128)S(1)} fusion(bf16[8192,1024]{1,0:T(8,128)(2,1)} %param.12, bf16[256,8192]{1,0:T(8,128)(2,1)} %all-gather.3.cloned.1.call-done, f32[8192]{0:T(1024)} %param.11, f32[256]{0:T(256)S(1)} %add_rsqrt_fusion), kind=kOutput, calls=%fused_computation.18 | convolution fusion | flops 4301520896 | bytes 22053888 | tf_op jit(solution)/shard_map/dot_general | solution.py:56
  124.3 0.9 slice_negate_fusion
  125.2 0.4 copy.104
  125.6 1.5 copy.105
  127.8 2.6 bitcast_reduce_fusion
  130.6 2.1 fusion.3
  132.8 2.5 fusion.17
  135.3 0.4 fusion.18
  136.2 1.2 slice-done.3
  137.4 6.7 %fusion.38 = f32[256,8192]{1,0:T(8,128)} fusion(bf16[1024,8192]{1,0:T(8,128)(2,1)S(1)} %bitcast.101, bf16[32,8,8,128]{3,2,1,0:T(8,128)(2,1)S(1)} %bitcast.109), kind=kOutput, calls=%fused_computation.40 | convolution fusion | flops 4294967296 | bytes 25690112 | tf_op jit(solution)/shard_map/dot_general | solution.py:125
  144.2 146.5 %reduce-scatter.2.cloned.1.call-done = f32[256,1024]{1,0:T(8,128)} async-done(((f32[256,8192]{1,0:T(8,128)}), f32[256,1024]{1,0:T(8,128)}) %reduce-scatter.2.cloned.1.call-update) | async-done | bytes 1048592 | tf_op jit(solution)/shard_map/reduce_scatter | solution.py:126
  290.7 2.1 convert_element_type.67
  293.3 7.8 %all-gather.5.cloned.1.call-done = bf16[512,1024]{1,0:T(8,128)(2,1)} async-done(((bf16[256,1024]{1,0:T(8,128)(2,1)}), bf16[512,1024]{1,0:T(8,128)(2,1)}) %all-gather.5.cloned.1.call-update) | async-done | bytes 1048592 | tf_op jit(solution)/shard_map/all_gather | solution.py:166
  301.1 1.8 gather_fusion.3
  302.9 1.0 fusion.37
  (62 shorter events, 3.5 us)
Async XLA Ops:
  6.5 98.9 %copy-start = (bf16[8192,128]{1,0:T(8,128)(2,1)S(1)}, bf16[8192,128]{1,0:T(8,128)(2,1)}, u32[]{:S(2)}) copy-start(bf16[8192,128]{1,0:T(8,128)(2,1)} %param.14) | copy-start | bytes 6291460
  6.5 95.8 %all-gather.3.cloned.1.call-start = ((), (), s32[]{:S(2)}) async-start(), calls=%async_computation.2 | async-start | bytes 4718592 | tf_op jit(solution)/shard_map/all_gather | solution.py:54
  11.1 49.9 %all-to-all-start = ((bf16[2,128,2,8,128]{4,1,0,2,3:T(8,128)(2,1)}), bf16[2,128,2,8,128]{4,1,0,2,3:T(8,128)(2,1)S(1)}, u32[]{:S(2)}, u32[]{:S(2)}) async-start(bf16[2,128,2,8,128]{4,1,0,2,3:T(8,128)(2,1)} %copy.87), calls=%async_computation | async-start | bytes 2097152 | tf_op jit(solution)/shard_map/all_to_all | solution.py:97
  18.4 272.2 %reduce-scatter.2.cloned.1.call-start = ((), (), s32[]{:S(2)}) async-start(), calls=%async_computation.3 | async-start | bytes 9437184 | tf_op jit(solution)/shard_map/reduce_scatter | solution.py:126
  62.1 47.6 %copy-start.6 = (f32[8192]{0:T(1024)S(1)}, f32[8192]{0:T(1024)}, u32[]{:S(2)}) copy-start(f32[8192]{0:T(1024)} %param.11) | copy-start | bytes 98308
  123.8 3.7 %copy-start.3 = (pred[128,128]{0,1:T(8,128)(4,1)S(1)}, pred[128,128]{0,1:T(8,128)(4,1)}, u32[]{:S(2)}) copy-start(pred[128,128]{0,1:T(8,128)(4,1)} %iota_compare_fusion) | copy-start | bytes 49156
  127.8 4.9 %copy-start.2 = (bf16[2,8,128,2,1,128]{5,2,1,0,3,4:T(8,128)(2,1)S(1)}, bf16[2,8,128,2,1,128]{5,2,1,0,3,4:T(8,128)(2,1)}, u32[]{:S(2)}) copy-start(bf16[2,8,128,2,1,128]{5,2,1,0,3,4:T(8,128)(2,1)} %copy.88) | copy-start | bytes 3145732
  130.6 5.4 %slice-start = ((s8[16777216]{0:T(1024)(128)(4,1)}), s8[4194304]{0:T(1024)(128)(4,1)S(1)}, s32[]{:S(2)}) async-start(s8[16777216]{0:T(1024)(128)(4,1)} %bitcast.100), calls=%async_computation.5 | async-start | bytes 8388608
  132.8 2.5 copy-start.4
  132.8 3.3 %slice-start.1 = ((s8[16777216]{0:T(1024)(128)(4,1)}), s8[4194304]{0:T(1024)(128)(4,1)S(1)}, s32[]{:S(2)}) async-start(s8[16777216]{0:T(1024)(128)(4,1)} %bitcast.100), calls=%async_computation.6 | async-start | bytes 8388608
  132.8 3.4 %slice-start.2 = ((s8[16777216]{0:T(1024)(128)(4,1)}), s8[4194304]{0:T(1024)(128)(4,1)S(1)}, s32[]{:S(2)}) async-start(s8[16777216]{0:T(1024)(128)(4,1)} %bitcast.100), calls=%async_computation.7 | async-start | bytes 8388608
  132.8 4.6 %slice-start.3 = ((s8[16777216]{0:T(1024)(128)(4,1)}), s8[4194304]{0:T(1024)(128)(4,1)S(1)}, s32[]{:S(2)}) async-start(s8[16777216]{0:T(1024)(128)(4,1)} %bitcast.100), calls=%async_computation.8 | async-start | bytes 8388608
  137.4 166.6 %copy-start.1 = (bf16[8192,128]{1,0:T(8,128)(2,1)S(1)}, bf16[8192,128]{1,0:T(8,128)(2,1)}, u32[]{:S(2)}) copy-start(bf16[8192,128]{1,0:T(8,128)(2,1)} %param.14) | copy-start | bytes 6291460
  144.1 148.7 %copy-start.5 = (s32[4]{0:T(128)S(1)}, s32[4]{0:T(128)}, u32[]{:S(2)}) copy-start(s32[4]{0:T(128)} %param.19) | copy-start | bytes 52
  144.2 156.9 %all-gather.5.cloned.1.call-start = ((), (), s32[]{:S(2)}) async-start(), calls=%async_computation.4 | async-start | bytes 1572864 | tf_op jit(solution)/shard_map/all_gather | solution.py:166
Sparse Core Ops, SparseCore 0:
  9.5 92.8 all-gather.2
  144.3 146.3 reduce-scatter.1
  292.9 8.1 all-gather.4
where the time goes:
time: 311 us; the launch traced here: 310 us
  waiting for transfers between devices  228 us (73%)
  matrix products  30 us (10%)
  local copies, waits for them, and re-layouts  19.5 us (6%)
  between operations  13.5 us (4%)
  other arithmetic  12.2 us (4%)
  starting transfers between devices  7.39 us (2%)
    reduce_scatter x1, waiting for transfers between devices, attend(): lax.psum_scatter(partial_value, 'tensor', scatter_dimension=1, tiled=True)  146 us
    all_gather x1, waiting for transfers between devices, attend(): lax.all_gather(token_rows, 'tensor', axis=1, tiled=True).astype(jnp.float32)  40.3 us
    all_to_all x1, waiting for transfers between devices, attend(): lax.all_to_all(spread, 'tensor', split_axis=3, concat_axis=1, tiled=True)  32.7 us
    dot_general x1, matrix products, attend(): jnp.dot(scaled, query_weight, preferred_element_type=jnp.float32)  9.52 us
    all_gather x1, waiting for transfers between devices, local(): everyone = lax.all_gather(mixed, 'worker', axis=0, tiled=True)  7.81 us
    all_to_all x1, starting transfers between devices, attend(): lax.all_to_all(spread, 'tensor', split_axis=3, concat_axis=1, tiled=True)  7.31 us
    dot_general x1, matrix products, attend(): jnp.dot(attended_rows, output_weight, preferred_element_type=jnp.float32)  6.74 us
  transfers between devices with their start and end apart: 4, of which 4 were waited for; matrix products, arithmetic and copies ran while one was open for 5% of the time, Pallas kernels for 0%

commit v1 on v0

--- a/solution.py
+++ b/solution.py
@@ -51,7 +51,9 @@
     seq_count = blocks.shape[0]
     total = token_rows.shape[0]
     query_cols = query_weight.shape[1]
-    widened = lax.all_gather(token_rows, "tensor", axis=1, tiled=True).astype(jnp.float32)
+    widened = jnp.concatenate(
+        lax.all_to_all(jnp.stack([token_rows] * lax.axis_size("tensor")), "tensor", 0, 0), axis=1
+    ).astype(jnp.float32)
     scaled = (widened * norm_gain[None, :]).astype(jnp.bfloat16)
     query_sum = jnp.dot(scaled, query_weight, preferred_element_type=jnp.float32)
     key_sum = jnp.dot(scaled, key_weight, preferred_element_type=jnp.float32)

time: 311 us -> 359 us (1.15)
  waiting for transfers between devices: 228 us -> 261 us
  local copies, waits for them, and re-layouts: 19.5 us -> 27.6 us
  starting transfers between devices: 7.39 us -> 12.1 us
  other arithmetic: 12.2 us -> 16.6 us
    all_to_all x0 -> x1, waiting for transfers between devices: none -> 82.8 us  [attend(): lax.all_to_all(jnp.stack([token_rows] * lax.axis_size('tensor')), 'tensor...]
    all_gather x1 -> x0, waiting for transfers between devices: 40.3 us -> none  [attend(): lax.all_gather(token_rows, 'tensor', axis=1, tiled=True).astype(jnp.float32)]
    all_to_all x1, waiting for transfers between devices: 32.7 us -> 23.7 us  [attend(): lax.all_to_all(spread, 'tensor', split_axis=3, concat_axis=1, tiled=True)]
    all_to_all x0 -> x1, starting transfers between devices: none -> 4.55 us  [attend(): lax.all_to_all(jnp.stack([token_rows] * lax.axis_size('tensor')), 'tensor...]
    unnamed x24 -> x29, local copies, waits for them, and re-layouts: 4.12 us -> 8.31 us
  transfers between devices with their start and end apart: 4 -> 4, of which waited for: 4 -> 4; matrix products, arithmetic and copies ran while one was open for 5% -> 3% of each run, Pallas kernels for 0% -> 0%
where the time goes in v1:
time: 359 us; the launch traced here: 358 us
  waiting for transfers between devices  261 us (73%)
  local copies, waits for them, and re-layouts  27.6 us (8%)
  matrix products  26.5 us (7%)
  other arithmetic  16.6 us (5%)
  between operations  13.8 us (4%)
  starting transfers between devices  12.1 us (3%)
    reduce_scatter x1, waiting for transfers between devices, attend(): lax.psum_scatter(partial_value, 'tensor', scatter_dimension=1, tiled=True)  147 us
    all_to_all x1, waiting for transfers between devices, attend(): lax.all_to_all(jnp.stack([token_rows] * lax.axis_size('tensor')), 'tensor...  82.8 us
    all_to_all x1, waiting for transfers between devices, attend(): lax.all_to_all(spread, 'tensor', split_axis=3, concat_axis=1, tiled=True)  23.7 us
    unnamed x29, local copies, waits for them, and re-layouts  8.31 us
    dot_general x1, matrix products, attend(): jnp.dot(scaled, query_weight, preferred_element_type=jnp.float32)  8.27 us
    all_gather x1, waiting for transfers between devices, local(): everyone = lax.all_gather(mixed, 'worker', axis=0, tiled=True)  7.79 us
    all_to_all x1, starting transfers between devices, attend(): lax.all_to_all(spread, 'tensor', split_axis=3, concat_axis=1, tiled=True)  7.44 us
  transfers between devices with their start and end apart: 4, of which 4 were waited for; matrix products, arithmetic and copies ran while one was open for 3% of the time, Pallas kernels for 0%

profile of v1, /device:TPU:0, one launch (start us, length us, event | category | flops | bytes accessed | tf_op | source)
XLA Modules:
  0.0 358.0 jit_solution(5096807249290649992)
XLA Ops:
  6.5 2.7 copy.91
  9.2 1.3 copy.92
  10.5 7.4 %all-to-all-start.1 = ((bf16[2,128,2,8,128]{4,1,0,2,3:T(8,128)(2,1)}), bf16[2,128,2,8,128]{4,1,0,2,3:T(8,128)(2,1)S(1)}, u32[]{:S(2)}, u32[]{:S(2)}) async-start(bf16[2,128,2,8,128]{4,1,0,2,3:T(8,128)(2,1)} %copy.92), calls=%async_computation.1 | async-start | bytes 2097152 | tf_op jit(solution)/shard_map/all_to_all | solution.py:99
  18.0 2.0 copy.86
  20.0 23.7 %all-to-all-done.1 = bf16[2,128,2,8,128]{4,1,0,2,3:T(8,128)(2,1)S(1)} async-done(((bf16[2,128,2,8,128]{4,1,0,2,3:T(8,128)(2,1)}), bf16[2,128,2,8,128]{4,1,0,2,3:T(8,128)(2,1)S(1)}, u32[]{:S(2)}, u32[]{:S(2)}) %all-to-all-start.1) | async-done | bytes 1048608 | tf_op jit(solution)/shard_map/all_to_all | solution.py:99
  43.8 3.3 stack.2
  47.0 4.6 %all-to-all-start = ((bf16[8,256,1024]{1,2,0:T(8,128)(2,1)}), bf16[8,256,1024]{1,2,0:T(8,128)(2,1)}, u32[]{:S(2)}, u32[]{:S(2)}) async-start(bf16[8,256,1024]{1,2,0:T(8,128)(2,1)} %stack.2), calls=%async_computation | async-start | bytes 8388608 | tf_op jit(solution)/shard_map/all_to_all | solution.py:55
  53.1 4.0 %gather_fusion.1 = s32[1024,2]{1,0:T(8,128)} fusion(s32[2,64]{0,1:T(8,128)S(1)} %copy.84, s32[1024]{0:T(1024)S(1)} %broadcast_clamp_fusion), kind=kCustom, calls=%fused_computation.1 | custom fusion | bytes 20480 | tf_op jit(solution)/shard_map/jit(_take)/gather | solution.py:104
  57.1 1.2 copy.85
  60.2 1.1 copy.93
  61.3 82.8 %all-to-all-done = bf16[8,256,1024]{1,2,0:T(8,128)(2,1)} async-done(((bf16[8,256,1024]{1,2,0:T(8,128)(2,1)}), bf16[8,256,1024]{1,2,0:T(8,128)(2,1)}, u32[]{:S(2)}, u32[]{:S(2)}) %all-to-all-start) | async-done | bytes 4194336 | tf_op jit(solution)/shard_map/all_to_all | solution.py:55
  144.1 3.3 multiply_reduce_fusion
  147.4 2.9 fusion
  150.3 1.9 copy-done.3
  152.3 1.0 fusion.11
  154.0 4.0 %fusion.10 = f32[256,128]{0,1:T(8,128)S(1)} fusion(bf16[256,8192]{0,1:T(8,128)(2,1)} %copy-done.3, bf16[8192,128]{1,0:T(8,128)(2,1)} %param.13, f32[256]{0:T(256)S(1)} %add_rsqrt_fusion), kind=kOutput, calls=%fused_computation.25 | convolution fusion | flops 536969216 | bytes 6423552 | tf_op jit(solution)/shard_map/dot_general | solution.py:59
  158.0 8.3 %convolution_multiply_fusion = f32[256,1024]{1,0:T(8,128)S(1)} fusion(bf16[256,8192]{0,1:T(8,128)(2,1)S(1)} %copy-done.4, bf16[8192,1024]{1,0:T(8,128)(2,1)} %param.12, f32[256]{0:T(256)S(1)} %add_rsqrt_fusion), kind=kOutput, calls=%fused_computation.14 | convolution fusion | flops 4295229440 | bytes 22021120 | tf_op jit(solution)/shard_map/dot_general | solution.py:58
  167.0 1.1 slice_negate_fusion
  168.1 1.5 copy.109
  169.6 2.4 copy.110
  171.9 1.6 fusion.13
  173.5 1.0 fusion.47
  174.5 2.6 bitcast_reduce_fusion
  177.3 2.1 fusion.2
  179.5 2.5 fusion.7
  182.9 1.2 slice-done.3
  184.1 6.8 %fusion.16 = f32[256,8192]{1,0:T(8,128)} fusion(bf16[1024,8192]{1,0:T(8,128)(2,1)S(1)} %bitcast.110, bf16[32,8,8,128]{3,2,1,0:T(8,128)(2,1)S(1)} %bitcast.118), kind=kOutput, calls=%fused_computation.36 | convolution fusion | flops 4294967296 | bytes 25690112 | tf_op jit(solution)/shard_map/dot_general | solution.py:127
  190.9 147.0 %reduce-scatter.2.cloned.1.call-done = f32[256,1024]{1,0:T(8,128)} async-done(((f32[256,8192]{1,0:T(8,128)}), f32[256,1024]{1,0:T(8,128)}) %reduce-scatter.2.cloned.1.call-update) | async-done | bytes 1048592 | tf_op jit(solution)/shard_map/reduce_scatter | solution.py:128
  337.9 2.1 convert_element_type.80
  340.5 7.8 %all-gather.2.cloned.1.call-done = bf16[512,1024]{1,0:T(8,128)(2,1)} async-done(((bf16[256,1024]{1,0:T(8,128)(2,1)}), bf16[512,1024]{1,0:T(8,128)(2,1)}) %all-gather.2.cloned.1.call-update) | async-done | bytes 1048592 | tf_op jit(solution)/shard_map/all_gather | solution.py:168
  348.3 1.8 gather_fusion.3
  350.2 1.0 fusion.15
  (68 shorter events, 6.2 us)
Async XLA Ops:
  6.5 145.7 %copy-start = (bf16[8192,128]{1,0:T(8,128)(2,1)S(1)}, bf16[8192,128]{1,0:T(8,128)(2,1)}, u32[]{:S(2)}) copy-start(bf16[8192,128]{1,0:T(8,128)(2,1)} %param.14) | copy-start | bytes 6291460
  10.5 41.1 %copy-start.2 = (s32[4]{0:T(128)S(1)}, s32[4]{0:T(128)}, u32[]{:S(2)}) copy-start(s32[4]{0:T(128)} %param.17) | copy-start | bytes 52
  10.5 41.8 %copy-start.7 = (s32[4,64]{1,0:T(4,128)S(1)}, s32[4,64]{1,0:T(4,128)}, u32[]{:S(2)}) copy-start(s32[4,64]{1,0:T(4,128)} %param.18) | copy-start | bytes 3076
  10.5 33.2 %all-to-all-start.1 = ((bf16[2,128,2,8,128]{4,1,0,2,3:T(8,128)(2,1)}), bf16[2,128,2,8,128]{4,1,0,2,3:T(8,128)(2,1)S(1)}, u32[]{:S(2)}, u32[]{:S(2)}) async-start(bf16[2,128,2,8,128]{4,1,0,2,3:T(8,128)(2,1)} %copy.92), calls=%async_computation.1 | async-start | bytes 2097152 | tf_op jit(solution)/shard_map/all_to_all | solution.py:99
  47.0 97.1 %all-to-all-start = ((bf16[8,256,1024]{1,2,0:T(8,128)(2,1)}), bf16[8,256,1024]{1,2,0:T(8,128)(2,1)}, u32[]{:S(2)}, u32[]{:S(2)}) async-start(bf16[8,256,1024]{1,2,0:T(8,128)(2,1)} %stack.2), calls=%async_computation | async-start | bytes 8388608 | tf_op jit(solution)/shard_map/all_to_all | solution.py:55
  51.6 286.3 %reduce-scatter.2.cloned.1.call-start = ((), (), s32[]{:S(2)}) async-start(), calls=%async_computation.3 | async-start | bytes 9437184 | tf_op jit(solution)/shard_map/reduce_scatter | solution.py:128
  150.3 1.9 copy-start.3
  154.0 4.1 %copy-start.4 = (bf16[256,8192]{0,1:T(8,128)(2,1)S(1)}, bf16[256,8192]{0,1:T(8,128)(2,1)}, u32[]{:S(2)}) copy-start(bf16[256,8192]{0,1:T(8,128)(2,1)} %copy-done.3) | copy-start | bytes 12582916
  174.5 4.9 %copy-start.5 = (bf16[2,8,128,2,1,128]{5,2,1,0,3,4:T(8,128)(2,1)S(1)}, bf16[2,8,128,2,1,128]{5,2,1,0,3,4:T(8,128)(2,1)}, u32[]{:S(2)}) copy-start(bf16[2,8,128,2,1,128]{5,2,1,0,3,4:T(8,128)(2,1)} %copy.93) | copy-start | bytes 3145732
  177.3 5.4 %slice-start = ((s8[16777216]{0:T(1024)(128)(4,1)}), s8[4194304]{0:T(1024)(128)(4,1)S(1)}, s32[]{:S(2)}) async-start(s8[16777216]{0:T(1024)(128)(4,1)} %bitcast.109), calls=%async_computation.5 | async-start | bytes 8388608
  179.5 2.5 copy-start.6
  179.5 3.3 slice-start.1
  179.5 3.4 slice-start.2
  179.5 4.6 %slice-start.3 = ((s8[16777216]{0:T(1024)(128)(4,1)}), s8[4194304]{0:T(1024)(128)(4,1)S(1)}, s32[]{:S(2)}) async-start(s8[16777216]{0:T(1024)(128)(4,1)} %bitcast.109), calls=%async_computation.8 | async-start | bytes 8388608
  184.1 167.1 %copy-start.1 = (bf16[8192,128]{1,0:T(8,128)(2,1)S(1)}, bf16[8192,128]{1,0:T(8,128)(2,1)}, u32[]{:S(2)}) copy-start(bf16[8192,128]{1,0:T(8,128)(2,1)} %param.14) | copy-start | bytes 6291460
  190.8 149.2 %copy-start.8 = (s32[4]{0:T(128)S(1)}, s32[4]{0:T(128)}, u32[]{:S(2)}) copy-start(s32[4]{0:T(128)} %param.19) | copy-start | bytes 52
  190.9 157.5 %all-gather.2.cloned.1.call-start = ((), (), s32[]{:S(2)}) async-start(), calls=%async_computation.4 | async-start | bytes 1572864 | tf_op jit(solution)/shard_map/all_gather | solution.py:168
Sparse Core Ops, SparseCore 0:
  191.0 146.9 reduce-scatter.1
  340.2 8.0 all-gather.1
